TPU v7x, 128 devices: a whole 4x4x4 slice. The times are simulated.
128 devices in a mesh: grp: 4 (over x_hi, core), vec: 32 (over z, y, x_lo).
Axes of the slice: x: 4 (x_hi: 2, x_lo: 2; x = x_hi * 2 + x_lo), y: 4, z: 4, core: 2. Of those that a mesh axis runs over, the one named last changes fastest.
Arguments:
- vv_vectors: bfloat16 [1280, 1000, 1000], P(('grp', 'vec')), may hold values from -0.1875 to 0.1875
- oo_vectors: bfloat16 [1280, 100, 100], P(('grp', 'vec')), may hold values from -0.625 to 0.625
- ov_slab: bfloat16 [1280, 1024], P(('grp', 'vec')), may hold values from -0.15625 to 0.15625
- amplitudes: bfloat16 [100, 1000], P('grp'), may hold values from -6 to 6
Outputs:
- sigma_slab: float32 [96000, 1024], P(('grp', 'vec'))
All inputs are finite; a program needn't handle non-finite values.
Results may differ from a plain program's by a relative error of at most 0.0029.
Values may be sent and summed in bfloat16 or wider, within the bound.
No kernel may reach another device: no remote copies, remote signals or barrier semaphores. Data moves between devices by JAX's collectives and lax.ppermute only.
A program may use at most 128 MiB of HBM per device.

v0:
```python
import jax
import jax.numpy as jnp
from jax import lax
from jax.sharding import PartitionSpec as P

NV = 1000
I_ROWS = 96


def laid_out(blocks, dim):
    dims = list(blocks.shape[1:])
    dims[dim] *= blocks.shape[0]
    return jnp.moveaxis(blocks, 0, dim).reshape(dims)


def from_everyone(array, axis):
    size = lax.axis_size(axis)
    return lax.all_to_all(
        jnp.broadcast_to(array[None], (size, *array.shape)), axis, 0, 0, tiled=True
    )


def collect(array, axis, dim):
    return laid_out(from_everyone(array, axis), dim)


def split_up(array, dim, size):
    dims = array.shape
    blocks = array.reshape(*dims[:dim], size, dims[dim] // size, *dims[dim + 1 :])
    return jnp.moveaxis(blocks, dim, 0)


def joined_exchange(array, axis, axes, splits, concats):
    sizes = [lax.axis_size(a) for a in axes]
    blocks = split_up(array, splits[0], sizes[0])
    blocks = jnp.moveaxis(split_up(blocks, splits[1] + 1, sizes[1]), 0, 1)
    inside = blocks.shape[2:]
    blocks = blocks.reshape(-1, *inside)
    blocks = lax.all_to_all(blocks, axis, split_axis=0, concat_axis=0, tiled=True)
    blocks = laid_out(blocks.reshape(*sizes, *inside), concats[0] + 1)
    return laid_out(blocks, concats[1])


def shards(vv_vectors, oo_vectors, ov_slab, amplitudes):
    amps_all = collect(amplitudes, "grp", 0)
    window = amps_all[:I_ROWS]
    local_count = vv_vectors.shape[0]
    direct_term = jnp.einsum("ib,pab->pia", window, vv_vectors, preferred_element_type=jnp.float32)
    hole_term = jnp.einsum(
        "pji,ja->pia", oo_vectors[:, :, :I_ROWS], amps_all, preferred_element_type=jnp.float32
    )
    dressed = (direct_term - hole_term).astype(jnp.bfloat16).reshape(local_count, I_ROWS * NV)
    regrouped = joined_exchange(dressed, ("grp", "vec"), ("grp", "vec"), (1, 1), (0, 0))
    group_slab = collect(ov_slab, "grp", 0)
    return lax.dot_general(
        regrouped,
        lax.all_gather(group_slab, "vec", axis=0, tiled=True),
        (((0,), (0,)), ((), ())),
        preferred_element_type=jnp.float32,
    )


def solution(mesh):
    return jax.shard_map(
        shards,
        mesh=mesh,
        in_specs=(
            P(("grp", "vec"), None, None),
            P(("grp", "vec"), None, None),
            P(("grp", "vec"), None),
            P("grp", None),
        ),
        out_specs=P(("grp", "vec"), None),
        check_vma=False,
    )
```

profile of v0, /device:TPU:4, one launch (start us, length us, event | category | flops | bytes accessed | tf_op | source)
XLA Modules:
  0.0 197.3 jit_solution(13646007314827454208)
XLA Ops:
  6.5 0.0 all-gather.2.cloned.1.call-start
  6.5 0.8 broadcast_in_dim.5
  7.3 7.6 %all_to_all.15 = bf16[4,10,1024]{2,1,0:T(8,128)(2,1)S(1)} all-to-all(bf16[4,10,1024]{2,1,0:T(8,128)(2,1)S(1)} %broadcast_in_dim.5), channel_id=1, replica_groups=mesh['grp'=4,'vec'=32] {'grp'}, dimensions={0} | all-to-all | bytes 163840 | tf_op jit(solution)/shard_map/all_to_all | solution.py:18
  14.9 0.7 reshape.21
  15.5 0.0 all-gather.2.cloned.1.call-update
  15.6 0.9 broadcast_in_dim.4
  16.4 9.9 %all_to_all.16 = bf16[4,25,1000]{2,1,0:T(8,128)(2,1)S(1)} all-to-all(bf16[4,25,1000]{2,1,0:T(8,128)(2,1)S(1)} %broadcast_in_dim.4), channel_id=1, replica_groups=mesh['grp'=4,'vec'=32] {'grp'}, dimensions={0} | all-to-all | bytes 400000 | tf_op jit(solution)/shard_map/all_to_all | solution.py:18
  26.3 0.1 reshape.17
  26.4 0.1 reshape.23
  26.5 0.0 copy-start
  26.5 10.3 %fusion.2 = f32[10,1000,96]{1,2,0:T(8,128)S(1)} fusion(bf16[10,1000,1000]{2,1,0:T(8,128)(2,1)} %param.4, bf16[100,1000]{1,0:T(8,128)(2,1)S(1)} %reshape.17), kind=kOutput, calls=%fused_computation.4 | convolution fusion | flops 1920000000 | bytes 24036608 | tf_op jit(solution)/shard_map/ib,pab->pia/dot_general | solution.py:48
  36.8 0.0 copy-done
  36.8 0.7 fusion
  37.6 4.3 %reshape_reshape.6 = bf16[10,4,24000]{2,1,0:T(4,128)(2,1)} reshape(bf16[10,96,1000]{2,1,0:T(8,128)(2,1)S(1)} %fusion) | data formatting | bytes 3840000 | tf_op jit(solution)/shard_map/reshape;reshape | solution.py:29
  41.9 6.0 %reshape.18 = bf16[4,10,32,750]{3,2,0,1:T(8,128)(2,1)S(1)} reshape(bf16[4,10,24000]{2,0,1:T(4,128)(2,1)} %bitcast.22) | data formatting | bytes 3840000 | tf_op jit(solution)/shard_map/reshape | solution.py:29
  47.9 1.2 copy.10
  49.1 70.7 %all_to_all.17 = bf16[128,10,750]{2,1,0:T(8,128)(2,1)S(1)} all-to-all(bf16[128,10,750]{2,1,0:T(8,128)(2,1)S(1)} %bitcast.20), channel_id=1, replica_groups=mesh['grp'=4,'vec'=32] {'grp','vec'}, dimensions={0} | all-to-all | bytes 3840000 | tf_op jit(solution)/shard_map/all_to_all | solution.py:39
  119.8 0.4 copy.12
  120.2 2.5 %reshape_reshape.7 = bf16[1280,750]{1,0:T(8,128)(2,1)} reshape(bf16[32,4,10,750]{3,2,1,0:T(8,128)(2,1)S(1)} %copy.12) | data formatting | bytes 3840000 | tf_op jit(solution)/shard_map/reshape;reshape | solution.py:13
  122.7 61.6 %all-gather.2.cloned.1.call-done = bf16[1280,1024]{1,0:T(8,128)(2,1)} async-done(((bf16[40,1024]{1,0:T(8,128)(2,1)}), bf16[1280,1024]{1,0:T(8,128)(2,1)}) %all-gather.2.cloned.1.call-update) | async-done | bytes 2621456 | tf_op jit(solution)/shard_map/all_gather | solution.py:57
  184.3 6.2 %fusion.3 = f32[750,1024]{1,0:T(8,128)} fusion(bf16[1280,750]{1,0:T(8,128)(2,1)} %reshape_reshape.7, bf16[1280,1024]{1,0:T(8,128)(2,1)} %all-gather.2.cloned.1.call-done), kind=kOutput, calls=%fused_computation.5 | convolution fusion | flops 1966080000 | bytes 7613440 | tf_op jit(solution)/shard_map/dot_general | solution.py:55
Async XLA Ops:
  6.5 177.8 %all-gather.2.cloned.1.call-start = ((), (), s32[]{:S(2)}) async-start(), calls=%async_computation.3 | async-start | bytes 2703360 | tf_op jit(solution)/shard_map/all_gather | solution.py:57
  26.5 10.3 %copy-start = (bf16[10,100,100]{2,1,0:T(8,128)(2,1)S(1)}, bf16[10,100,100]{2,1,0:T(8,128)(2,1)}, u32[]{:S(2)}) copy-start(bf16[10,100,100]{2,1,0:T(8,128)(2,1)} %param.5) | copy-start | bytes 600004
Sparse Core Ops, SparseCore 0:
  15.7 168.5 all-gather.1
where the time goes:
time: 198 us; the launch traced here: 197 us
  blocking collectives  88.1 us (44%)
  waiting for transfers between devices  61.6 us (31%)
  matrix products  17.2 us (9%)
  local copies, waits for them, and re-layouts  16.9 us (9%)
  between operations  13.5 us (7%)
    all_to_all x1, blocking collectives, joined_exchange(): lax.all_to_all(blocks, axis, split_axis=0, concat_axis=0, tiled=True)  70.7 us
    all_gather x1, waiting for transfers between devices, shards(): lax.all_gather(group_slab, 'vec', axis=0, tiled=True)  61.6 us
    all_to_all x2, blocking collectives, from_everyone(): lax.all_to_all(jnp.broadcast_to(array[None], (size, *array.shape)), axis,...  17.5 us
    dot_general x1, matrix products, shards(): jnp.einsum('ib,pab->pia', window, vv_vectors, preferred_element_type=jnp....  10.3 us
    reshape x2, local copies, waits for them, and re-layouts, split_up(): array.reshape(*dims[:dim], size, dims[dim] // size, *dims[dim + 1:])  7.22 us
    dot_general x1, matrix products, shards(): lax.dot_general(regrouped, lax.all_gather(group_slab, 'vec', axis=0, tile...  6.16 us
    another operation x1, local copies, waits for them, and re-layouts, split_up(): array.reshape(*dims[:dim], size, dims[dim] // size, *dims[dim + 1:])  4.33 us
  transfers between devices with their start and end apart: 1, of which 1 were waited for; matrix products, arithmetic and copies ran while one was open for 13% of the time, Pallas kernels for 0%

commit v1 on v0

--- a/solution.py
+++ b/solution.py
@@ -54,7 +54,9 @@
     group_slab = collect(ov_slab, "grp", 0)
     return lax.dot_general(
         regrouped,
-        lax.all_gather(group_slab, "vec", axis=0, tiled=True),
+        jnp.concatenate(
+            lax.all_to_all(jnp.stack([group_slab] * lax.axis_size("vec")), "vec", 0, 0), axis=0
+        ),
         (((0,), (0,)), ((), ())),
         preferred_element_type=jnp.float32,
     )

time: 198 us -> 148 us (0.75)
  blocking collectives: 88.1 us -> 8.97 us
  starting transfers between devices: 0.01 us -> 21.7 us
  between operations: 13.5 us -> 0.08 us
  waiting for transfers between devices: 61.6 us -> 71.4 us
  local copies, waits for them, and re-layouts: 16.9 us -> 23.5 us
  matrix products: 17.2 us -> 20.8 us
    all_to_all x0 -> x3, waiting for transfers between devices: none -> 71.4 us  [the longest x1 40.6 us: joined_exchange(): lax.all_to_all(blocks, axis, split_axis=0, concat_axis=0, tiled=True)]
    all_to_all x1 -> x0, blocking collectives: 70.7 us -> none  [joined_exchange(): lax.all_to_all(blocks, axis, split_axis=0, concat_axis=0, tiled=True)]
    all_gather x1 -> x0, waiting for transfers between devices: 61.6 us -> none  [shards(): lax.all_gather(group_slab, 'vec', axis=0, tiled=True)]
    all_to_all x0 -> x3, starting transfers between devices: none -> 21.7 us  [the longest x1 10.5 us: joined_exchange(): lax.all_to_all(blocks, axis, split_axis=0, concat_axis=0, tiled=True)]
    all_to_all x2 -> x1, blocking collectives: 17.5 us -> 8.97 us  [from_everyone(): lax.all_to_all(jnp.broadcast_to(array[None], (size, *array.shape)), axis,...]
    dot_general x1, matrix products: 0.72 us -> 2.83 us  [shards(): jnp.einsum('pji,ja->pia', oo_vectors[:, :, :I_ROWS], amps_all, preferred_...]
    dot_general x1, matrix products: 10.3 us -> 12.4 us  [shards(): jnp.einsum('ib,pab->pia', window, vv_vectors, preferred_element_type=jnp....]
  transfers between devices with their start and end apart: 1 -> 3, of which waited for: 1 -> 2; matrix products, arithmetic and copies ran while one was open for 13% -> 24% of each run, Pallas kernels for 0% -> 0%
where the time goes in v1:
time: 148 us; the launch traced here: 146 us
  waiting for transfers between devices  71.4 us (48%)
  local copies, waits for them, and re-layouts  23.5 us (16%)
  starting transfers between devices  21.7 us (15%)
  matrix products  20.8 us (14%)
  blocking collectives  8.97 us (6%)
    all_to_all x1, waiting for transfers between devices, joined_exchange(): lax.all_to_all(blocks, axis, split_axis=0, concat_axis=0, tiled=True)  40.6 us
    all_to_all x1, waiting for transfers between devices, shards(): lax.all_to_all(jnp.stack([group_slab] * lax.axis_size('vec')), 'vec', 0, 0)  30.8 us
    dot_general x1, matrix products, shards(): jnp.einsum('ib,pab->pia', window, vv_vectors, preferred_element_type=jnp....  12.4 us
    all_to_all x1, starting transfers between devices, joined_exchange(): lax.all_to_all(blocks, axis, split_axis=0, concat_axis=0, tiled=True)  10.5 us
    all_to_all x1, blocking collectives, from_everyone(): lax.all_to_all(jnp.broadcast_to(array[None], (size, *array.shape)), axis,...  8.97 us
    reshape x2, local copies, waits for them, and re-layouts, split_up(): array.reshape(*dims[:dim], size, dims[dim] // size, *dims[dim + 1:])  8.87 us
    all_to_all x1, starting transfers between devices, from_everyone(): lax.all_to_all(jnp.broadcast_to(array[None], (size, *array.shape)), axis,...  6.43 us
    dot_general x1, matrix products, shards(): lax.dot_general(regrouped, jnp.concatenate(lax.all_to_all(jnp.stack([grou...  5.57 us
  transfers between devices with their start and end apart: 3, of which 2 were waited for; matrix products, arithmetic and copies ran while one was open for 24% of the time, Pallas kernels for 0%

profile of v1, /device:TPU:4, one launch (start us, length us, event | category | flops | bytes accessed | tf_op | source)
XLA Modules:
  0.0 146.5 jit_solution(1865740219389505840)
XLA Ops:
  0.0 0.9 broadcast_in_dim.4
  0.9 9.0 %all_to_all.20 = bf16[4,25,1000]{2,1,0:T(8,128)(2,1)S(1)} all-to-all(bf16[4,25,1000]{2,1,0:T(8,128)(2,1)S(1)} %broadcast_in_dim.4), channel_id=1, replica_groups=mesh['grp'=4,'vec'=32] {'grp'}, dimensions={0} | all-to-all | bytes 400000 | tf_op jit(solution)/shard_map/all_to_all | solution.py:18
  9.8 1.4 broadcast_in_dim.5
  11.3 6.4 %all-to-all-start.2 = ((bf16[4,10,1024]{2,1,0:T(8,128)(2,1)}), bf16[4,10,1024]{2,1,0:T(8,128)(2,1)S(1)}, u32[]{:S(2)}, u32[]{:S(2)}) async-start(bf16[4,10,1024]{2,1,0:T(8,128)(2,1)} %broadcast_in_dim.5), calls=%async_computation.2 | async-start | bytes 262144 | tf_op jit(solution)/shard_map/all_to_all | solution.py:18
  17.7 0.1 reshape.19
  17.8 0.0 copy-start
  17.8 12.4 %fusion.2 = f32[10,1000,96]{1,2,0:T(8,128)} fusion(bf16[10,1000,1000]{2,1,0:T(8,128)(2,1)} %param.4, bf16[100,1000]{1,0:T(8,128)(2,1)S(1)} %reshape.19), kind=kOutput, calls=%fused_computation.4 | convolution fusion | flops 1920000000 | bytes 24036608 | tf_op jit(solution)/shard_map/ib,pab->pia/dot_general | solution.py:48
  30.2 0.1 reshape.25
  30.2 0.0 copy-done
  30.3 2.8 %fusion = bf16[10,96,1000]{2,1,0:T(8,128)(2,1)S(1)} fusion(f32[10,1000,96]{1,2,0:T(8,128)} %fusion.2, bf16[100,1000,1]{1,0,2:T(8,128)(2,1)S(1)} %reshape.25, bf16[10,100,100]{2,1,0:T(8,128)(2,1)S(1)} %copy-done), kind=kOutput, calls=%fused_computation.1 | convolution fusion | flops 193920000 | bytes 6160000 | tf_op jit(solution)/shard_map/pji,ja->pia/dot_general | solution.py:49
  33.1 4.3 %reshape_reshape.6 = bf16[10,4,24000]{2,1,0:T(4,128)(2,1)} reshape(bf16[10,96,1000]{2,1,0:T(8,128)(2,1)S(1)} %fusion) | data formatting | bytes 3840000 | tf_op jit(solution)/shard_map/reshape;reshape | solution.py:29
  37.4 6.0 %reshape.20 = bf16[4,10,32,750]{3,2,0,1:T(8,128)(2,1)S(1)} reshape(bf16[4,10,24000]{2,0,1:T(4,128)(2,1)} %bitcast.23) | data formatting | bytes 3840000 | tf_op jit(solution)/shard_map/reshape | solution.py:29
  43.5 2.8 %copy.10 = bf16[4,10,32,750]{3,1,2,0:T(8,128)(2,1)} copy(bf16[4,10,32,750]{3,2,0,1:T(8,128)(2,1)S(1)} %reshape.20) | data formatting | bytes 3840000 | tf_op jit(solution)/shard_map/reshape | solution.py:29
  46.3 0.0 all-to-all-done.2
  46.3 10.5 %all-to-all-start.1 = ((bf16[128,10,750]{2,1,0:T(8,128)(2,1)}), bf16[128,10,750]{2,1,0:T(8,128)(2,1)S(1)}, u32[]{:S(2)}, u32[]{:S(2)}) async-start(bf16[128,10,750]{2,1,0:T(8,128)(2,1)} %bitcast.22), calls=%async_computation.1 | async-start | bytes 6291456 | tf_op jit(solution)/shard_map/all_to_all | solution.py:39
  56.9 40.6 %all-to-all-done.1 = bf16[128,10,750]{2,1,0:T(8,128)(2,1)S(1)} async-done(((bf16[128,10,750]{2,1,0:T(8,128)(2,1)}), bf16[128,10,750]{2,1,0:T(8,128)(2,1)S(1)}, u32[]{:S(2)}, u32[]{:S(2)}) %all-to-all-start.1) | async-done | bytes 1920032 | tf_op jit(solution)/shard_map/all_to_all | solution.py:39
  97.4 1.8 %stack.3 = bf16[32,40,1024]{2,1,0:T(8,128)(2,1)} broadcast(bf16[40,1024]{1,0:T(8,128)(2,1)S(1)} %stack_reshape.2), dimensions={1,2} | broadcast | bytes 2703360 | tf_op jit(solution)/shard_map/stack | solution.py:58
  99.2 4.8 %all-to-all-start.3 = ((bf16[32,40,1024]{2,1,0:T(8,128)(2,1)}), bf16[32,40,1024]{2,1,0:T(8,128)(2,1)}, u32[]{:S(2)}, u32[]{:S(2)}) async-start(bf16[32,40,1024]{2,1,0:T(8,128)(2,1)} %stack.3), calls=%async_computation.3 | async-start | bytes 5242880 | tf_op jit(solution)/shard_map/all_to_all | solution.py:58
  104.0 2.1 %copy.12 = bf16[32,4,10,750]{3,2,1,0:T(8,128)(2,1)} copy(bf16[32,4,10,750]{3,2,0,1:T(8,128)(2,1)S(1)} %bitcast.21) | data formatting | bytes 3840000 | tf_op jit(solution)/shard_map/transpose | solution.py:13
  106.1 3.9 %reshape_reshape.7 = bf16[1280,750]{1,0:T(8,128)(2,1)S(1)} reshape(bf16[32,4,10,750]{3,2,1,0:T(8,128)(2,1)} %copy.12) | data formatting | bytes 3840000 | tf_op jit(solution)/shard_map/reshape;reshape | solution.py:13
  110.1 30.8 %all-to-all-done.3 = bf16[32,40,1024]{2,1,0:T(8,128)(2,1)} async-done(((bf16[32,40,1024]{2,1,0:T(8,128)(2,1)}), bf16[32,40,1024]{2,1,0:T(8,128)(2,1)}, u32[]{:S(2)}, u32[]{:S(2)}) %all-to-all-start.3) | async-done | bytes 2621472 | tf_op jit(solution)/shard_map/all_to_all | solution.py:58
  140.9 5.6 %fusion.3 = f32[750,1024]{1,0:T(8,128)} fusion(bf16[1280,750]{1,0:T(8,128)(2,1)S(1)} %reshape_reshape.7, bf16[1280,1024]{1,0:T(8,128)(2,1)} %bitcast.8), kind=kOutput, calls=%fused_computation.5 | convolution fusion | flops 1966080000 | bytes 7613440 | tf_op jit(solution)/shard_map/dot_general | solution.py:55
  (1 shorter events, 0.0 us)
Async XLA Ops:
  11.3 35.0 %all-to-all-start.2 = ((bf16[4,10,1024]{2,1,0:T(8,128)(2,1)}), bf16[4,10,1024]{2,1,0:T(8,128)(2,1)S(1)}, u32[]{:S(2)}, u32[]{:S(2)}) async-start(bf16[4,10,1024]{2,1,0:T(8,128)(2,1)} %broadcast_in_dim.5), calls=%async_computation.2 | async-start | bytes 262144 | tf_op jit(solution)/shard_map/all_to_all | solution.py:18
  17.8 12.5 %copy-start = (bf16[10,100,100]{2,1,0:T(8,128)(2,1)S(1)}, bf16[10,100,100]{2,1,0:T(8,128)(2,1)}, u32[]{:S(2)}) copy-start(bf16[10,100,100]{2,1,0:T(8,128)(2,1)} %param.5) | copy-start | bytes 600004
  46.3 51.1 %all-to-all-start.1 = ((bf16[128,10,750]{2,1,0:T(8,128)(2,1)}), bf16[128,10,750]{2,1,0:T(8,128)(2,1)S(1)}, u32[]{:S(2)}, u32[]{:S(2)}) async-start(bf16[128,10,750]{2,1,0:T(8,128)(2,1)} %bitcast.22), calls=%async_computation.1 | async-start | bytes 6291456 | tf_op jit(solution)/shard_map/all_to_all | solution.py:39
  99.2 41.6 %all-to-all-start.3 = ((bf16[32,40,1024]{2,1,0:T(8,128)(2,1)}), bf16[32,40,1024]{2,1,0:T(8,128)(2,1)}, u32[]{:S(2)}, u32[]{:S(2)}) async-start(bf16[32,40,1024]{2,1,0:T(8,128)(2,1)} %stack.3), calls=%async_computation.3 | async-start | bytes 5242880 | tf_op jit(solution)/shard_map/all_to_all | solution.py:58
